TPU v7x, 32 devices: a whole 2x2x4 slice. The times are simulated.
32 devices in a mesh: dir: 8 (over y, x, core), freq: 4 (over z).
Axes of the slice: x: 2, y: 2, z: 4, core: 2. Of those that a mesh axis runs over, the one named last changes fastest.
Arguments:
- observed: float32 [512, 8, 2, 2, 512], P('dir', 'freq'), as said below
- flags: int32 [512, 2, 512], P('dir'), may hold values from 0 to 1, as said below
- screen: float32 [16, 512], P('dir'), may hold values from -6 to 6
- screen_kernel: float32 [512, 512], replicated
- station_uv: float32 [2, 2, 512], replicated, may hold values from -360 to 360
- source_lm: float32 [2, 3072], P(None, 'dir'), may hold values from -0.05 to 0.05
- source_flux: float32 [3072], P('dir')
- station_gain: bfloat16 [8, 2, 2, 512, 3072], P('freq', None, None, None, 'dir'), may hold values from -4.1875 to 4.1875
- source_direction: int32 [3072], P('dir'), may hold values from 0 to 1
- freq_ratio: float32 [8], P('freq')
Outputs:
- residual: float32 [512, 8, 2, 2, 512], P('dir', 'freq')
- updated_screen: float32 [16, 512], P('dir')
Inputs may be any that keep to these rules, and one draw needn't show every extreme that they name: observed is Hermitian in its stations: observed[p, f, t, 0, q] equals observed[q, f, t, 0, p] and observed[p, f, t, 1, q] equals minus observed[q, f, t, 1, p]. flags[p, t, q] equals flags[q, t, p].
All inputs are finite; a program needn't handle non-finite values.
Results may differ from a plain program's by a relative error of at most 0.0037.
Values may be sent and summed in bfloat16 or wider, within the bound.
A program may use at most 128 MiB of HBM per device.

v0:
```python
import math
import jax
import jax.numpy as jnp
from jax import lax
from jax.sharding import PartitionSpec as P

step_size = 0.3
epsilon = 1e-06
highest = lax.Precision.HIGHEST


def body(
    observed,
    flags,
    screen,
    screen_kernel,
    station_uv,
    source_lm,
    source_flux,
    station_gain,
    source_direction,
    freq_ratio,
):
    dir_count = lax.axis_size("dir")
    stations = screen.shape[1]
    local_dirs = screen.shape[0]
    local_sources = source_flux.shape[0]
    local_rows = observed.shape[0]
    channels = freq_ratio.shape[0]
    times_count = station_uv.shape[0]
    matrices = channels * times_count
    scaling = 1.0 / math.sqrt(local_sources * dir_count)
    onehot_dirs = (
        source_direction[:, None] == jnp.arange(local_dirs, dtype=jnp.int32)[None, :]
    ).astype(jnp.float32)
    screen_src = jnp.einsum("dp,kd->pk", screen, onehot_dirs, precision=highest)
    freq_each = jnp.repeat(freq_ratio, times_count)
    uv_each = jnp.tile(station_uv, (channels, 1, 1))
    geometry = jnp.einsum("mcp,ck->pmk", uv_each, source_lm, precision=highest)
    phase_angle = (
        screen_src[:, None, :] / freq_each[None, :, None]
        + (2.0 * math.pi * freq_each)[None, :, None] * geometry
    )
    gain_all = station_gain.reshape(matrices, 2, stations, local_sources).astype(jnp.float32)
    gain_re = jnp.transpose(gain_all[:, 0], (1, 0, 2))
    gain_im = jnp.transpose(gain_all[:, 1], (1, 0, 2))
    cosine = jnp.cos(phase_angle)
    sine = jnp.sin(phase_angle)
    amplitude = jnp.sqrt(source_flux)[None, None, :]
    phasor_re = (amplitude * (gain_re * cosine - gain_im * sine)).astype(jnp.bfloat16)
    phasor_im = (amplitude * (gain_re * sine + gain_im * cosine)).astype(jnp.bfloat16)
    left_mat = jnp.concatenate([phasor_re, phasor_im], axis=2)
    skew_mat = jnp.concatenate([phasor_im, -phasor_re], axis=2)
    real_part = jnp.einsum("pmk,qmk->pmq", left_mat, left_mat, preferred_element_type=jnp.float32)
    imag_part = jnp.einsum("pmk,qmk->pmq", skew_mat, left_mat, preferred_element_type=jnp.float32)
    packed_rows = lax.psum_scatter(
        (real_part + imag_part) * scaling, "dir", scatter_dimension=0, tiled=True
    )
    mirrored = lax.all_to_all(packed_rows, "dir", split_axis=2, concat_axis=0, tiled=True)
    mirrored = jnp.transpose(mirrored, (2, 1, 0))
    model_rows = jnp.stack([(packed_rows + mirrored) * 0.5, (packed_rows - mirrored) * 0.5], axis=2)
    row_ids = lax.axis_index("dir") * local_rows + jnp.arange(local_rows, dtype=jnp.int32)
    cross_baseline = (row_ids[:, None] != jnp.arange(stations, dtype=jnp.int32)[None, :]).astype(
        jnp.float32
    )
    baseline_keep = (
        jnp.tile(flags, (1, channels, 1)).astype(jnp.float32) * cross_baseline[:, None, :]
    )
    obs_rows = observed.reshape(local_rows, matrices, 2, stations)
    residual = baseline_keep[:, :, None, :] * (obs_rows - model_rows)
    resid_half = residual.astype(jnp.bfloat16)
    forward_mat = jnp.stack([left_mat, -skew_mat], axis=2)
    conj_mat = jnp.concatenate([phasor_re, -phasor_im], axis=2)
    dual_mat = jnp.concatenate([phasor_im, phasor_re], axis=2)
    adjoint_mat = jnp.stack([conj_mat, dual_mat], axis=2)
    rows_piece = lax.all_gather(resid_half, "dir", axis=0, tiled=True)
    row_part = jnp.einsum(
        "rmwq,qmwk->rmk", rows_piece, forward_mat, preferred_element_type=jnp.float32
    )
    col_total = jnp.einsum(
        "rmwp,rmwk->pmk", rows_piece, adjoint_mat, preferred_element_type=jnp.float32
    )
    weight_re = row_part[..., :local_sources] + col_total[..., :local_sources]
    weight_im = row_part[..., local_sources:] - col_total[..., local_sources:]
    source_grad = (
        phasor_im.astype(jnp.float32) * weight_re - phasor_re.astype(jnp.float32) * weight_im
    )
    source_grad = source_grad * (scaling / freq_each)[None, :, None]
    local_grad = jnp.einsum("pmk,kd->dp", source_grad, onehot_dirs, precision=highest)
    entry_count = local_dirs * dir_count * stations
    total_grad = lax.psum(local_grad, "freq")
    smooth = jnp.dot(total_grad, screen_kernel, precision=highest)
    total_sq = lax.psum(jnp.sum(smooth * smooth), "dir")
    updated = screen - step_size * smooth * lax.rsqrt(total_sq / entry_count + epsilon)
    return (residual.reshape(observed.shape), updated)


def solution(mesh):
    placed = (
        P("dir", "freq", None, None, None),
        P("dir", None, None),
        P("dir", None),
        P(),
        P(),
        P(None, "dir"),
        P("dir"),
        P("freq", None, None, None, "dir"),
        P("dir"),
        P("freq"),
    )
    return jax.shard_map(
        body,
        mesh=mesh,
        in_specs=placed,
        out_specs=(P("dir", "freq", None, None, None), P("dir", None)),
        check_vma=False,
    )
```

profile of v0, /device:TPU:0, one launch (start us, length us, event | category | flops | bytes accessed | tf_op | source)
XLA Modules:
  0.0 248.1 jit_solution(14236749292300200952)
XLA Ops:
  7.2 0.0 copy-start
  7.2 0.0 all-reduce.3.cloned.1.call-start
  7.2 0.8 broadcast_in_dim.2
  8.0 0.1 div.26
  8.1 0.7 sqrt.3
  8.8 0.0 copy-start.12
  8.8 5.5 %copy.27 = f32[2,2,2,512,384]{3,4,1,0,2:T(8,128)} copy(bf16[2,2,2,512,384]{4,3,2,1,0:T(8,128)(2,1)} %param.17) | data formatting | bytes 9437184 | tf_op jit(solution)/shard_map/convert_element_type | solution.py:44
  14.3 0.0 copy-done.9
  14.3 0.0 copy-done.10
  14.3 0.5 convolution_bitcast_fusion
  14.8 0.0 copy-done.11
  14.8 0.0 slice-start
  14.9 0.0 copy-done.12
  14.9 0.0 slice-start.1
  14.9 14.2 %fusion.46 = (f32[512,4,384]{0,2,1:T(8,128)S(1)}, f32[512,4,384]{0,2,1:T(8,128)S(1)}) fusion(f32[4,2,512]{2,1,0:T(2,128)S(1)} %bitcast.86, f32[2,384]{1,0:T(2,128)S(1)} %copy-done.12, f32[4]{0:T(128)S(1)} %get-tuple-element.16, f32[4]{0:T(128)S(1)} %div.26, f32[512,384]{0,1:T(8,128)S(1)} %convolution_bitcast_fusion), kind=kOutput, calls=%fused_computation.68 | convolution fusion | flops 21233664 | bytes 7097376 | tf_op jit(solution)/shard_map/mcp,ck->pmk/dot_general | solution.py:39
  29.1 3.2 %fusion.45 = (bf16[512,4,384]{0,2,1:T(8,128)(2,1)}, bf16[512,4,384]{0,2,1:T(8,128)(2,1)S(1)}, bf16[512,4,1,384]{0,3,1,2:T(8,128)(2,1)}, bf16[512,4,384]{0,2,1:T(8,128)(2,1)S(1)}) fusion(f32[512,4,384]{0,2,1:T(8,128)S(1)} %get-tuple-element.10, f32[4,2,512,384]{2,3,0,1:T(8,128)S(1)} %bitcast.78, f32[512,4,384]{0,2,1:T(8,128)S(1)} %get-tuple-element.11, ...), kind=kLoop, calls=%fused_computation.67 | loop fusion | flops 9437184 | bytes 18875904 | tf_op jit(solution)/shard_map/neg | solution.py:73
  32.3 0.3 neg.16
  32.6 2.1 fusion.30
  34.7 3.5 %multiply_bitcast_fusion = f32[512,4,512]{0,2,1:T(8,128)} fusion(f32[4,512,512]{2,1,0:T(8,128)S(1)} %fusion.30, bf16[512,4,384]{0,2,1:T(8,128)(2,1)S(1)} %get-tuple-element.5, bf16[512,4,384]{0,2,1:T(8,128)(2,1)S(1)} %neg.16, bf16[512,4,384]{0,2,1:T(8,128)(2,1)S(1)} %get-tuple-element.7), kind=kOutput, calls=%fused_computation.8 | convolution fusion | flops 1625292800 | bytes 13107200 | tf_op jit(solution)/shard_map/pmk,qmk->pmq/dot_general | solution.py:55
  38.1 5.5 %copy.32 = f32[512,4,512]{2,1,0:T(4,128)} copy(f32[512,4,512]{0,2,1:T(8,128)} %multiply_bitcast_fusion) | data formatting | bytes 8388608 | tf_op jit(solution)/shard_map/mul | solution.py:57
  43.6 0.0 all-reduce.3.cloned.1.call-update
  43.6 0.9 copy-done.8
  44.6 0.1 convert_element_type.42
  44.6 0.1 tile.6
  44.8 1.3 convert_element_type.49
  46.0 0.6 dynamic-slice
  47.3 80.0 %all-reduce.3.cloned.1.call-done = f32[512,4,512]{2,1,0:T(4,128)} async-done(((f32[512,4,512]{2,1,0:T(4,128)}), f32[512,4,512]{2,1,0:T(4,128)}) %all-reduce.3.cloned.1.call-update) | async-done | bytes 4194320
  127.3 1.1 constant_dynamic-slice_fusion
  128.4 1.3 copy.33
  129.7 3.0 %reshape.106 = f32[8,1,16384]{2,1,0:T(1,128)} reshape(f32[512,4,64]{2,1,0:T(4,128)} %bitcast.83) | data formatting | bytes 1048576
  132.7 3.5 %all-to-all-start = ((f32[8,1,16384]{2,1,0:T(1,128)}), f32[8,1,16384]{2,1,0:T(1,128)S(1)}, u32[]{:S(2)}, u32[]{:S(2)}) async-start(f32[8,1,16384]{2,1,0:T(1,128)} %reshape.106), calls=%async_computation | async-start | bytes 1048576 | tf_op jit(solution)/shard_map/all_to_all | solution.py:59
  136.2 0.2 all-gather.2.cloned.1.call-start
  136.4 0.1 fusion.37
  136.5 2.0 broadcast_multiply_fusion
  138.5 7.4 %all-to-all-done = f32[8,1,16384]{2,1,0:T(1,128)S(1)} async-done(((f32[8,1,16384]{2,1,0:T(1,128)}), f32[8,1,16384]{2,1,0:T(1,128)S(1)}, u32[]{:S(2)}, u32[]{:S(2)}) %all-to-all-start) | async-done | bytes 524320 | tf_op jit(solution)/shard_map/all_to_all | solution.py:59
  145.9 0.8 copy-done.7
  146.7 0.5 broadcast.60
  147.2 2.9 %reduce = f32[8,16384]{1,0:T(8,128)S(1)} reduce(f32[8,1,16384]{2,1,0:T(1,128)} %copy-done.7, f32[]{:T(128)} %broadcast.60), dimensions={1}, to_apply=%all_to_all.13.reduce_sub_computation | reduce | bytes 1048580 | tf_op jit(solution)/shard_map/all_to_all | solution.py:59
  150.1 1.7 reshape.107
  151.8 2.8 %copy.64 = f32[64,4,8,64]{0,2,1,3:T(8,128)} copy(f32[64,4,8,64]{0,1,3,2:T(4,128)} %bitcast.84) | data formatting | bytes 1048576 | tf_op jit(solution)/shard_map/all_to_all | solution.py:59
  154.6 2.4 all_to_all.16
  156.9 1.4 fusion.34
  158.4 0.0 copy-start.5
  158.4 0.8 copy-done.5
  159.2 1.8 fusion.33
  161.0 1.0 copy.38
  161.9 0.0 all-gather.2.cloned.1.call-update
  162.0 4.4 %maximum_negate_fusion = bf16[512,4,1,768]{0,3,1,2:T(8,128)(2,1)} fusion(bf16[512,4,1,384]{0,3,1,2:T(8,128)(2,1)} %get-tuple-element.6, bf16[512,4,1,384]{0,3,1,2:T(8,128)(2,1)} %bitcast.79), kind=kLoop, calls=%fused_computation.29 | loop fusion | flops 7864320 | bytes 6291456 | tf_op jit(solution)/shard_map/neg | solution.py:72
  166.3 1.0 broadcast_multiply_fusion.1
  167.3 3.8 %fusion.29 = (bf16[512,4,1,768]{0,3,1,2:T(8,128)(2,1)}, bf16[512,4,1,768]{0,3,1,2:T(8,128)(2,1)}, bf16[512,4,1,768]{0,3,1,2:T(8,128)(2,1)}) fusion(bf16[512,4,384]{0,2,1:T(8,128)(2,1)S(1)} %copy-done.2, bf16[512,4,384]{0,2,1:T(8,128)(2,1)S(1)} %get-tuple-element.7, bf16[512,4,384]{0,2,1:T(8,128)(2,1)S(1)} %copy-done.4), kind=kLoop, calls=%fused_computation.34 | loop fusion | flops 17301504 | bytes 14155776 | tf_op jit(solution)/shard_map/stack | solution.py:72
  171.1 2.6 %stack.42 = f32[64,2,2,1,512]{4,3,2,1,0:T(1,128)} reshape(f32[64,4,512]{2,1,0:T(4,128)} %copy-done.5) | data formatting | bytes 1048576 | tf_op jit(solution)/shard_map/stack | solution.py:61
  173.7 1.5 stack.43
  175.2 3.9 %fusion.31 = f32[64,2,2,2,512]{4,3,2,1,0:T(2,128)} fusion(f32[64,2,2,2,512]{4,3,2,1,0:T(2,128)} %param.10, f32[64,2,2,1,512]{4,3,2,1,0:T(1,128)} %stack.43, f32[64,2,2,1,512]{4,3,2,1,0:T(1,128)} %stack.42, f32[64,2,2,512]{3,2,1,0:T(2,128)} %broadcast_multiply_fusion.1), kind=kLoop, calls=%fused_computation.38 | loop fusion | flops 786432 | bytes 3670016 | tf_op jit(solution)/shard_map/mul | solution.py:70
  179.1 18.7 %all-gather.2.cloned.1.call-done = bf16[512,4,2,512]{3,1,2,0:T(4,128)(2,1)} async-done(((bf16[64,4,2,512]{3,1,2,0:T(4,128)(2,1)}), bf16[512,4,2,512]{3,1,2,0:T(4,128)(2,1)}) %all-gather.2.cloned.1.call-update) | async-done | bytes 4194320 | tf_op jit(solution)/shard_map/all_gather | solution.py:76
  197.8 7.7 %fusion.24 = f32[512,4,768]{0,2,1:T(8,128)S(1)} fusion(bf16[512,4,2,512]{3,1,2,0:T(4,128)(2,1)} %all-gather.2.cloned.1.call-done, bf16[512,4,1,768]{0,3,1,2:T(8,128)(2,1)} %maximum_negate_fusion, bf16[512,4,1,768]{0,3,1,2:T(8,128)(2,1)} %get-tuple-element.8), kind=kOutput, calls=%fused_computation.33 | convolution fusion | flops 3224371200 | bytes 16777216 | tf_op jit(solution)/shard_map/rmwq,qmwk->rmk/dot_general | solution.py:77
  205.5 0.0 copy-done.6
  205.5 0.0 copy-start.3
  205.5 6.8 %fusion.19 = f32[512,4,768]{0,2,1:T(8,128)S(1)} fusion(bf16[512,4,2,512]{3,1,2,0:T(4,128)(2,1)} %all-gather.2.cloned.1.call-done, bf16[512,4,1,768]{0,3,1,2:T(8,128)(2,1)S(1)} %copy-done.6, bf16[512,4,1,768]{0,3,1,2:T(8,128)(2,1)} %get-tuple-element.12), kind=kOutput, calls=%fused_computation.32 | convolution fusion | flops 3224371200 | bytes 16777216 | tf_op jit(solution)/shard_map/rmwp,rmwk->pmk/dot_general | solution.py:80
  212.3 1.9 fusion.16
  214.2 0.4 fusion.36
  214.7 11.7 %psum.14 = f32[2,512]{1,0:T(2,128)S(1)} all-reduce(f32[2,512]{1,0:T(2,128)S(1)} %fusion.36), channel_id=1, replica_groups=mesh['dir'=8,'freq'=4] {'freq'}, use_global_device_ids=true, to_apply=%region_2.0 | all-reduce | flops 1024 | bytes 8192 | tf_op jit(solution)/shard_map/psum | solution.py:91
  226.3 1.2 multiply_reduce_fusion
  227.5 12.5 %psum.15 = f32[]{:T(128)} all-reduce(f32[]{:T(128)} %get-tuple-element.18), channel_id=1, replica_groups=mesh['dir'=8,'freq'=4] {'dir'}, use_global_device_ids=true, to_apply=%region_4.0 | all-reduce | flops 1 | bytes 8 | tf_op jit(solution)/shard_map/psum | solution.py:93
  240.7 0.6 multiply_subtract_fusion
  (22 shorter events, 0.1 us)
Async XLA Ops:
  7.2 219.2 %copy-start = (f32[512,512]{1,0:T(8,128)S(1)}, f32[512,512]{1,0:T(8,128)}, u32[]{:S(2)}) copy-start(f32[512,512]{1,0:T(8,128)} %param.13) | copy-start | bytes 3145732
  7.2 120.1 %all-reduce.3.cloned.1.call-start = ((), (), s32[]{:S(2)}) async-start(), calls=%async_computation.2 | async-start | bytes 8388608
  8.8 5.5 %copy-start.9 = (f32[2,512]{1,0:T(2,128)S(1)}, f32[2,512]{1,0:T(2,128)}, u32[]{:S(2)}) copy-start(f32[2,512]{1,0:T(2,128)} %param.12) | copy-start | bytes 12292
  8.8 5.5 %copy-start.10 = (s32[384]{0:T(512)S(1)}, s32[384]{0:T(512)}, u32[]{:S(2)}) copy-start(s32[384]{0:T(512)} %param.18) | copy-start | bytes 4612
  8.8 6.0 %copy-start.11 = (f32[2,2,512]{2,1,0:T(2,128)S(1)}, f32[2,2,512]{2,1,0:T(2,128)}, u32[]{:S(2)}) copy-start(f32[2,2,512]{2,1,0:T(2,128)} %param.14) | copy-start | bytes 24580
  8.8 6.0 %copy-start.12 = (f32[2,384]{1,0:T(2,128)S(1)}, f32[2,384]{1,0:T(2,128)}, u32[]{:S(2)}) copy-start(f32[2,384]{1,0:T(2,128)} %param.15) | copy-start | bytes 9220
  14.8 14.2 %slice-start = ((s8[6291456]{0:T(1024)(128)(4,1)}), s8[4194304]{0:T(1024)(128)(4,1)S(1)}, s32[]{:S(2)}) async-start(s8[6291456]{0:T(1024)(128)(4,1)} %bitcast.76), calls=%async_computation.3 | async-start | bytes 8388608
  14.9 14.2 %slice-start.1 = ((s8[6291456]{0:T(1024)(128)(4,1)}), s8[2097152]{0:T(1024)(128)(4,1)S(1)}, s32[]{:S(2)}) async-start(s8[6291456]{0:T(1024)(128)(4,1)} %bitcast.76), calls=%async_computation.4 | async-start | bytes 4194304
  32.3 2.4 copy-start.1
  43.6 0.9 copy-start.8
  43.6 2.4 copy-start.13
  132.7 13.1 %all-to-all-start = ((f32[8,1,16384]{2,1,0:T(1,128)}), f32[8,1,16384]{2,1,0:T(1,128)S(1)}, u32[]{:S(2)}, u32[]{:S(2)}) async-start(f32[8,1,16384]{2,1,0:T(1,128)} %reshape.106), calls=%async_computation | async-start | bytes 1048576 | tf_op jit(solution)/shard_map/all_to_all | solution.py:59
  136.2 61.6 %all-gather.2.cloned.1.call-start = ((), (), s32[]{:S(2)}) async-start(), calls=%async_computation.1 | async-start | bytes 4718592 | tf_op jit(solution)/shard_map/all_gather | solution.py:76
  145.9 0.8 copy-start.7
  158.4 0.8 copy-start.5
  161.9 5.4 %copy-start.2 = (bf16[512,4,384]{0,2,1:T(8,128)(2,1)S(1)}, bf16[512,4,384]{0,2,1:T(8,128)(2,1)}, u32[]{:S(2)}) copy-start(bf16[512,4,384]{0,2,1:T(8,128)(2,1)} %copy-done.1) | copy-start | bytes 4718596
  162.0 5.4 %copy-start.4 = (bf16[512,4,384]{0,2,1:T(8,128)(2,1)S(1)}, bf16[512,4,384]{0,2,1:T(8,128)(2,1)}, u32[]{:S(2)}) copy-start(bf16[512,4,384]{0,2,1:T(8,128)(2,1)} %get-tuple-element.4) | copy-start | bytes 4718596
  197.8 7.8 %copy-start.6 = (bf16[512,4,1,768]{0,3,1,2:T(8,128)(2,1)S(1)}, bf16[512,4,1,768]{0,3,1,2:T(8,128)(2,1)}, u32[]{:S(2)}) copy-start(bf16[512,4,1,768]{0,3,1,2:T(8,128)(2,1)} %get-tuple-element.9) | copy-start | bytes 9437188
  205.5 6.8 %copy-start.3 = (bf16[512,4,384]{0,2,1:T(8,128)(2,1)S(1)}, bf16[512,4,384]{0,2,1:T(8,128)(2,1)}, u32[]{:S(2)}) copy-start(bf16[512,4,384]{0,2,1:T(8,128)(2,1)} %copy-done.1) | copy-start | bytes 4718596
Sparse Core Ops, SparseCore 0:
  43.8 83.5 all-reduce.2
  162.1 35.6 all-gather.1
where the time goes:
time: 249 us; the launch traced here: 248 us
  waiting for transfers between devices  106 us (43%)
  matrix products  36.4 us (15%)
  local copies, waits for them, and re-layouts  34.8 us (14%)
  other arithmetic  27.3 us (11%)
  blocking collectives  24.1 us (10%)
  between operations  15.6 us (6%)
  starting transfers between devices  3.75 us (2%)
    unnamed x3, waiting for transfers between devices  80.1 us
    all_gather x1, waiting for transfers between devices, body(): rows_piece = lax.all_gather(resid_half, 'dir', axis=0, tiled=True)  18.7 us
    dot_general x1, matrix products, body(): geometry = jnp.einsum('mcp,ck->pmk', uv_each, source_lm, precision=highest)  14.2 us
    psum x1, blocking collectives, body(): total_sq = lax.psum(jnp.sum(smooth * smooth), 'dir')  12.5 us
    psum x1, blocking collectives, body(): total_grad = lax.psum(local_grad, 'freq')  11.7 us
    unnamed x36, local copies, waits for them, and re-layouts  8.85 us
    dot_general x1, matrix products, body(): jnp.einsum('rmwq,qmwk->rmk', rows_piece, forward_mat, preferred_element_t...  7.74 us
    all_to_all x1, waiting for transfers between devices, body(): lax.all_to_all(packed_rows, 'dir', split_axis=2, concat_axis=0, tiled=True)  7.36 us
  transfers between devices with their start and end apart: 3, of which 3 were waited for; matrix products, arithmetic and copies ran while one was open for 9% of the time, Pallas kernels for 0%

commit v1 on v0

--- a/solution.py
+++ b/solution.py
@@ -3,6 +3,7 @@
 import jax.numpy as jnp
 from jax import lax
 from jax.sharding import PartitionSpec as P
+from jax.lax import axis_index, ppermute, psum
 
 step_size = 0.3
 epsilon = 1e-06
@@ -73,7 +74,15 @@
     conj_mat = jnp.concatenate([phasor_re, -phasor_im], axis=2)
     dual_mat = jnp.concatenate([phasor_im, phasor_re], axis=2)
     adjoint_mat = jnp.stack([conj_mat, dual_mat], axis=2)
-    rows_piece = lax.all_gather(resid_half, "dir", axis=0, tiled=True)
+    lanes = psum(1, "dir")
+    r_now = [(kk - 1, kk) for kk in range(1, lanes)] + [(lanes - 1, 0)]
+    prior = resid_half
+    nodes = [prior]
+    for _ in range(lanes - 1):
+        prior = ppermute(prior, "dir", r_now)
+        nodes += [prior]
+    block_now = jnp.concatenate([*reversed(nodes)], 0)
+    rows_piece = jnp.roll(block_now, (axis_index("dir") + 1) * prior.shape[0], 0)
     row_part = jnp.einsum(
         "rmwq,qmwk->rmk", rows_piece, forward_mat, preferred_element_type=jnp.float32
     )

time: 249 us -> 287 us (1.15)
  waiting for transfers between devices: 106 us -> 142 us
  local copies, waits for them, and re-layouts: 34.8 us -> 41.2 us
  other arithmetic: 27.3 us -> 24 us
    ppermute x0 -> x7, waiting for transfers between devices: none -> 57 us  [body(): prior = ppermute(prior, 'dir', r_now)]
    all_gather x1 -> x0, waiting for transfers between devices: 18.7 us -> none  [body(): rows_piece = lax.all_gather(resid_half, 'dir', axis=0, tiled=True)]
    unnamed x36 -> x69, local copies, waits for them, and re-layouts: 8.85 us -> 21.3 us
    all_to_all x1, waiting for transfers between devices: 7.36 us -> 2.99 us  [body(): lax.all_to_all(packed_rows, 'dir', split_axis=2, concat_axis=0, tiled=True)]
    another operation x2, local copies, waits for them, and re-layouts: 4.08 us -> 1.08 us  [body(): jnp.stack([(packed_rows + mirrored) * 0.5, (packed_rows - mirrored) * 0.5...]
    unnamed x3 -> x2, waiting for transfers between devices: 80.1 us -> 81.9 us
  transfers between devices with their start and end apart: 3 -> 9, of which waited for: 3 -> 9; matrix products, arithmetic and copies ran while one was open for 9% -> 6% of each run, Pallas kernels for 0% -> 0%
where the time goes in v1:
time: 287 us; the launch traced here: 286 us
  waiting for transfers between devices  142 us (49%)
  local copies, waits for them, and re-layouts  41.2 us (14%)
  matrix products  34.7 us (12%)
  blocking collectives  24.1 us (8%)
  other arithmetic  24 us (8%)
  between operations  15.9 us (6%)
  starting transfers between devices  4.45 us (2%)
    unnamed x2, waiting for transfers between devices  81.9 us
    ppermute x7, waiting for transfers between devices, body(): prior = ppermute(prior, 'dir', r_now)  57 us
    unnamed x69, local copies, waits for them, and re-layouts  21.3 us
    dot_general x1, matrix products, body(): geometry = jnp.einsum('mcp,ck->pmk', uv_each, source_lm, precision=highest)  14.2 us
    psum x1, blocking collectives, body(): total_sq = lax.psum(jnp.sum(smooth * smooth), 'dir')  12.4 us
    psum x1, blocking collectives, body(): total_grad = lax.psum(local_grad, 'freq')  11.7 us
    dot_general x1, matrix products, body(): jnp.einsum('rmwp,rmwk->pmk', rows_piece, adjoint_mat, preferred_element_t...  7.47 us
  transfers between devices with their start and end apart: 9, of which 9 were waited for; matrix products, arithmetic and copies ran while one was open for 6% of the time, Pallas kernels for 0%

profile of v1, /device:TPU:0, one launch (start us, length us, event | category | flops | bytes accessed | tf_op | source)
XLA Modules:
  0.0 286.2 jit_solution(10706411373598960313)
XLA Ops:
  7.2 0.0 copy-start
  7.2 0.0 all-reduce.3.cloned.1.call-start
  7.2 0.8 broadcast_in_dim.2
  8.0 0.1 div.26
  8.1 0.0 copy-start.18
  8.1 0.0 copy-start.20
  8.2 5.5 %copy.27 = f32[2,2,2,512,384]{3,4,1,0,2:T(8,128)} copy(bf16[2,2,2,512,384]{4,3,2,1,0:T(8,128)(2,1)} %param.17) | data formatting | bytes 9437184 | tf_op jit(solution)/shard_map/convert_element_type | solution.py:45
  13.7 0.5 convolution_bitcast_fusion
  14.2 14.2 %fusion.46 = (f32[512,4,384]{0,2,1:T(8,128)S(1)}, f32[512,4,384]{0,2,1:T(8,128)S(1)}) fusion(f32[4,2,512]{2,1,0:T(2,128)S(1)} %bitcast.94, f32[2,384]{1,0:T(2,128)S(1)} %copy-done.20, f32[4]{0:T(128)S(1)} %get-tuple-element.16, f32[4]{0:T(128)S(1)} %div.26, f32[512,384]{0,1:T(8,128)S(1)} %convolution_bitcast_fusion), kind=kOutput, calls=%fused_computation.85 | convolution fusion | flops 21233664 | bytes 7097376 | tf_op jit(solution)/shard_map/mcp,ck->pmk/dot_general | solution.py:40
  28.4 3.3 %fusion.45 = (bf16[512,4,384]{0,2,1:T(8,128)(2,1)}, bf16[512,4,384]{0,2,1:T(8,128)(2,1)S(1)}, bf16[512,4,1,384]{0,3,1,2:T(8,128)(2,1)}, bf16[512,4,384]{0,2,1:T(8,128)(2,1)S(1)}) fusion(f32[512,4,384]{0,2,1:T(8,128)S(1)} %get-tuple-element.10, f32[4,2,512,384]{2,3,0,1:T(8,128)S(1)} %bitcast.85, f32[512,4,384]{0,2,1:T(8,128)S(1)} %get-tuple-element.11, ...), kind=kLoop, calls=%fused_computation.84 | loop fusion | flops 9437184 | bytes 18875904 | tf_op jit(solution)/shard_map/neg | solution.py:74
  31.7 0.3 neg.16
  32.0 2.1 fusion.30
  34.1 3.5 %multiply_bitcast_fusion = f32[512,4,512]{0,2,1:T(8,128)} fusion(f32[4,512,512]{2,1,0:T(8,128)S(1)} %fusion.30, bf16[512,4,384]{0,2,1:T(8,128)(2,1)S(1)} %get-tuple-element.5, bf16[512,4,384]{0,2,1:T(8,128)(2,1)S(1)} %neg.16, bf16[512,4,384]{0,2,1:T(8,128)(2,1)S(1)} %get-tuple-element.7), kind=kOutput, calls=%fused_computation.8 | convolution fusion | flops 1625292800 | bytes 13107200 | tf_op jit(solution)/shard_map/pmk,qmk->pmq/dot_general | solution.py:56
  37.6 5.4 %copy.32 = f32[512,4,512]{2,1,0:T(4,128)} copy(f32[512,4,512]{0,2,1:T(8,128)} %multiply_bitcast_fusion) | data formatting | bytes 8388608 | tf_op jit(solution)/shard_map/mul | solution.py:58
  43.1 0.0 all-reduce.3.cloned.1.call-update
  43.1 0.6 copy-done.21
  43.7 0.6 dynamic-slice
  44.9 81.8 %all-reduce.3.cloned.1.call-done = f32[512,4,512]{2,1,0:T(4,128)} async-done(((f32[512,4,512]{2,1,0:T(4,128)}), f32[512,4,512]{2,1,0:T(4,128)}) %all-reduce.3.cloned.1.call-update) | async-done | bytes 4194320
  126.8 1.1 constant_dynamic-slice_fusion
  127.9 1.3 copy.33
  129.2 3.0 %reshape.106 = f32[8,1,16384]{2,1,0:T(1,128)} reshape(f32[512,4,64]{2,1,0:T(4,128)} %bitcast.91) | data formatting | bytes 1048576
  132.2 4.3 %all-to-all-start = ((f32[8,1,16384]{2,1,0:T(1,128)}), f32[8,1,16384]{2,1,0:T(1,128)}, u32[]{:S(2)}, u32[]{:S(2)}) async-start(f32[8,1,16384]{2,1,0:T(1,128)} %reshape.106), calls=%async_computation | async-start | bytes 1048576 | tf_op jit(solution)/shard_map/all_to_all | solution.py:60
  136.5 1.0 convert_element_type.42
  137.6 0.8 copy.51
  138.3 2.9 copy.40
  141.2 0.1 fusion.37
  141.3 1.8 bitcast_multiply_fusion
  143.1 3.0 %all-to-all-done = f32[8,1,16384]{2,1,0:T(1,128)} async-done(((f32[8,1,16384]{2,1,0:T(1,128)}), f32[8,1,16384]{2,1,0:T(1,128)}, u32[]{:S(2)}, u32[]{:S(2)}) %all-to-all-start) | async-done | bytes 524320 | tf_op jit(solution)/shard_map/all_to_all | solution.py:60
  146.1 0.5 broadcast.61
  146.6 3.7 %reduce = f32[8,16384]{1,0:T(8,128)} reduce(f32[8,1,16384]{2,1,0:T(1,128)} %all-to-all-done, f32[]{:T(128)} %broadcast.61), dimensions={1}, to_apply=%all_to_all.13.reduce_sub_computation | reduce | bytes 1048580 | tf_op jit(solution)/shard_map/all_to_all | solution.py:60
  150.3 2.7 reshape.107
  153.0 2.8 copy.63
  155.8 2.3 all_to_all.16
  158.1 1.3 fusion.34
  159.4 2.0 fusion.33
  161.4 0.1 collective-permute-start
  161.5 9.5 %collective-permute-done = bf16[64,4,2,512]{3,0,2,1:T(8,128)(2,1)S(1)} collective-permute-done((bf16[64,4,2,512]{3,0,2,1:T(8,128)(2,1)S(1)}, bf16[64,4,2,512]{3,0,2,1:T(8,128)(2,1)S(1)}, u32[]{:S(2)}, u32[]{:S(2)}) %collective-permute-start) | collective-permute-done | bytes 524320 | tf_op jit(solution)/shard_map/ppermute | solution.py:82
  171.0 9.5 %collective-permute-done.1 = bf16[64,4,2,512]{3,0,2,1:T(8,128)(2,1)S(1)} collective-permute-done((bf16[64,4,2,512]{3,0,2,1:T(8,128)(2,1)S(1)}, bf16[64,4,2,512]{3,0,2,1:T(8,128)(2,1)S(1)}, u32[]{:S(2)}, u32[]{:S(2)}) %collective-permute-start.1) | collective-permute-done | bytes 524320 | tf_op jit(solution)/shard_map/ppermute | solution.py:82
  180.5 0.8 copy-done.11
  181.3 8.7 %collective-permute-done.2 = bf16[64,4,2,512]{3,0,2,1:T(8,128)(2,1)S(1)} collective-permute-done((bf16[64,4,2,512]{3,0,2,1:T(8,128)(2,1)S(1)}, bf16[64,4,2,512]{3,0,2,1:T(8,128)(2,1)S(1)}, u32[]{:S(2)}, u32[]{:S(2)}) %collective-permute-start.2) | collective-permute-done | bytes 524320 | tf_op jit(solution)/shard_map/ppermute | solution.py:82
  190.0 0.8 copy-done.13
  190.8 9.6 %collective-permute-done.3 = bf16[64,4,2,512]{3,0,2,1:T(8,128)(2,1)} collective-permute-done((bf16[64,4,2,512]{3,0,2,1:T(8,128)(2,1)S(1)}, bf16[64,4,2,512]{3,0,2,1:T(8,128)(2,1)}, u32[]{:S(2)}, u32[]{:S(2)}) %collective-permute-start.3) | collective-permute-done | bytes 524320 | tf_op jit(solution)/shard_map/ppermute | solution.py:82
  200.4 9.8 %collective-permute-done.4 = bf16[64,4,2,512]{3,0,2,1:T(8,128)(2,1)} collective-permute-done((bf16[64,4,2,512]{3,0,2,1:T(8,128)(2,1)}, bf16[64,4,2,512]{3,0,2,1:T(8,128)(2,1)}, u32[]{:S(2)}, u32[]{:S(2)}) %collective-permute-start.4) | collective-permute-done | bytes 524320 | tf_op jit(solution)/shard_map/ppermute | solution.py:82
  210.2 2.5 maximum_negate_fusion
  212.8 3.1 %fusion.29 = (bf16[512,4,1,768]{0,3,1,2:T(8,128)(2,1)S(1)}, bf16[512,4,1,768]{0,3,1,2:T(8,128)(2,1)}, bf16[512,4,1,768]{0,3,1,2:T(8,128)(2,1)}) fusion(bf16[512,4,384]{0,2,1:T(8,128)(2,1)S(1)} %copy-done.2, bf16[512,4,384]{0,2,1:T(8,128)(2,1)S(1)} %get-tuple-element.7, bf16[512,4,384]{0,2,1:T(8,128)(2,1)S(1)} %copy-done.3), kind=kLoop, calls=%fused_computation.34 | loop fusion | flops 17301504 | bytes 14155776 | tf_op jit(solution)/shard_map/stack | solution.py:73
  215.9 4.0 %collective-permute-done.5 = bf16[64,4,2,512]{3,0,2,1:T(8,128)(2,1)S(1)} collective-permute-done((bf16[64,4,2,512]{3,0,2,1:T(8,128)(2,1)}, bf16[64,4,2,512]{3,0,2,1:T(8,128)(2,1)S(1)}, u32[]{:S(2)}, u32[]{:S(2)}) %collective-permute-start.5) | collective-permute-done | bytes 524320 | tf_op jit(solution)/shard_map/ppermute | solution.py:82
  219.9 0.2 broadcast_multiply_fusion
  220.1 0.5 copy.37
  220.7 0.5 copy.38
  221.3 2.3 fusion.31
  223.6 5.9 %collective-permute-done.6 = bf16[64,4,2,512]{3,0,2,1:T(8,128)(2,1)S(1)} collective-permute-done((bf16[64,4,2,512]{3,0,2,1:T(8,128)(2,1)S(1)}, bf16[64,4,2,512]{3,0,2,1:T(8,128)(2,1)S(1)}, u32[]{:S(2)}, u32[]{:S(2)}) %collective-permute-start.6) | collective-permute-done | bytes 524320 | tf_op jit(solution)/shard_map/ppermute | solution.py:82
  229.5 1.1 constant_dynamic-update-slice_fusion.13
  230.6 1.1 constant_dynamic-update-slice_fusion.12
  232.1 1.1 constant_dynamic-update-slice_fusion.5
  233.1 1.1 constant_dynamic-update-slice_fusion.4
  234.5 3.3 %copy-done.15 = bf16[1024,4,2,512]{3,0,2,1:T(8,128)(2,1)} copy-done((bf16[1024,4,2,512]{3,0,2,1:T(8,128)(2,1)}, bf16[1024,4,2,512]{3,0,2,1:T(8,128)(2,1)S(1)}, u32[]{:S(2)}) %copy-start.15) | copy-done | bytes 8388632
  237.7 5.3 %fusion.24 = f32[512,4,768]{0,2,1:T(8,128)S(1)} fusion(bf16[512,4,1,768]{0,3,1,2:T(8,128)(2,1)S(1)} %maximum_negate_fusion, bf16[512,4,1,768]{0,3,1,2:T(8,128)(2,1)S(1)} %get-tuple-element.8, bf16[1024,4,2,512]{3,0,2,1:T(8,128)(2,1)} %copy-done.15, s32[]{:T(128)S(6)} %select_n.14), kind=kOutput, calls=%fused_computation.33 | convolution fusion | flops 3224371200 | bytes 16777220 | tf_op jit(solution)/shard_map/rmwq,qmwk->rmk/dot_general | solution.py:86
  243.0 7.5 %fusion.19 = f32[512,4,768]{0,2,1:T(8,128)S(1)} fusion(bf16[512,4,1,768]{0,3,1,2:T(8,128)(2,1)} %get-tuple-element.9, bf16[512,4,1,768]{0,3,1,2:T(8,128)(2,1)} %get-tuple-element.12, bf16[1024,4,2,512]{3,0,2,1:T(8,128)(2,1)} %copy-done.15, s32[]{:T(128)S(6)} %select_n.14), kind=kOutput, calls=%fused_computation.32 | convolution fusion | flops 3224371200 | bytes 16777220 | tf_op jit(solution)/shard_map/rmwp,rmwk->pmk/dot_general | solution.py:89
  250.5 1.9 fusion.16
  252.3 0.4 fusion.36
  252.8 11.7 %psum.14 = f32[2,512]{1,0:T(2,128)S(1)} all-reduce(f32[2,512]{1,0:T(2,128)S(1)} %fusion.36), channel_id=1, replica_groups=mesh['dir'=8,'freq'=4] {'freq'}, use_global_device_ids=true, to_apply=%region_2.3 | all-reduce | flops 1024 | bytes 8192 | tf_op jit(solution)/shard_map/psum | solution.py:100
  264.5 1.2 multiply_reduce_fusion
  265.7 12.4 %psum.15 = f32[]{:T(128)} all-reduce(f32[]{:T(128)} %get-tuple-element.18), channel_id=1, replica_groups=mesh['dir'=8,'freq'=4] {'dir'}, use_global_device_ids=true, to_apply=%region_4.5 | all-reduce | flops 1 | bytes 8 | tf_op jit(solution)/shard_map/psum | solution.py:102
  278.8 0.6 multiply_subtract_fusion
  (64 shorter events, 0.6 us)
Async XLA Ops:
  7.2 257.3 %copy-start = (f32[512,512]{1,0:T(8,128)S(1)}, f32[512,512]{1,0:T(8,128)}, u32[]{:S(2)}) copy-start(f32[512,512]{1,0:T(8,128)} %param.13) | copy-start | bytes 3145732
  7.2 119.6 %all-reduce.3.cloned.1.call-start = ((), (), s32[]{:S(2)}) async-start(), calls=%async_computation.1 | async-start | bytes 8388608
  8.1 5.5 %copy-start.19 = (f32[384]{0:T(512)S(1)}, f32[384]{0:T(512)}, u32[]{:S(2)}) copy-start(f32[384]{0:T(512)} %param.16) | copy-start | bytes 4612
  8.1 5.5 %copy-start.16 = (f32[2,512]{1,0:T(2,128)S(1)}, f32[2,512]{1,0:T(2,128)}, u32[]{:S(2)}) copy-start(f32[2,512]{1,0:T(2,128)} %param.12) | copy-start | bytes 12292
  8.1 5.5 %copy-start.17 = (s32[384]{0:T(512)S(1)}, s32[384]{0:T(512)}, u32[]{:S(2)}) copy-start(s32[384]{0:T(512)} %param.18) | copy-start | bytes 4612
  8.1 6.1 %copy-start.18 = (f32[2,2,512]{2,1,0:T(2,128)S(1)}, f32[2,2,512]{2,1,0:T(2,128)}, u32[]{:S(2)}) copy-start(f32[2,2,512]{2,1,0:T(2,128)} %param.14) | copy-start | bytes 24580
  8.1 6.1 %copy-start.20 = (f32[2,384]{1,0:T(2,128)S(1)}, f32[2,384]{1,0:T(2,128)}, u32[]{:S(2)}) copy-start(f32[2,384]{1,0:T(2,128)} %param.15) | copy-start | bytes 9220
  14.2 14.2 %slice-start = ((s8[6291456]{0:T(1024)(128)(4,1)}), s8[4194304]{0:T(1024)(128)(4,1)S(1)}, s32[]{:S(2)}) async-start(s8[6291456]{0:T(1024)(128)(4,1)} %bitcast.83), calls=%async_computation.2 | async-start | bytes 8388608
  14.2 14.2 %slice-start.1 = ((s8[6291456]{0:T(1024)(128)(4,1)}), s8[2097152]{0:T(1024)(128)(4,1)S(1)}, s32[]{:S(2)}) async-start(s8[6291456]{0:T(1024)(128)(4,1)} %bitcast.83), calls=%async_computation.3 | async-start | bytes 4194304
  31.7 2.4 copy-start.1
  43.1 0.7 copy-start.21
  132.2 13.9 %all-to-all-start = ((f32[8,1,16384]{2,1,0:T(1,128)}), f32[8,1,16384]{2,1,0:T(1,128)}, u32[]{:S(2)}, u32[]{:S(2)}) async-start(f32[8,1,16384]{2,1,0:T(1,128)} %reshape.106), calls=%async_computation | async-start | bytes 1048576 | tf_op jit(solution)/shard_map/all_to_all | solution.py:60
  159.3 11.6 %copy-start.4 = (f32[64,4,512]{2,0,1:T(8,128)}, f32[64,4,512]{2,0,1:T(8,128)S(1)}, u32[]{:S(2)}) copy-start(f32[64,4,512]{2,0,1:T(8,128)S(1)} %get-tuple-element.14) | copy-start | bytes 1572868
  159.4 11.6 %copy-start.6 = (f32[64,4,512]{2,0,1:T(8,128)}, f32[64,4,512]{2,0,1:T(8,128)S(1)}, u32[]{:S(2)}) copy-start(f32[64,4,512]{2,0,1:T(8,128)S(1)} %get-tuple-element.13) | copy-start | bytes 1572868
  161.4 9.6 %collective-permute-start = (bf16[64,4,2,512]{3,0,2,1:T(8,128)(2,1)S(1)}, bf16[64,4,2,512]{3,0,2,1:T(8,128)(2,1)S(1)}, u32[]{:S(2)}, u32[]{:S(2)}) collective-permute-start(bf16[64,4,2,512]{3,0,2,1:T(8,128)(2,1)S(1)} %fusion.33), channel_id=1, source_target_pairs={{0,4},{4,8},{8,12},{12,16},{16,20},{20,24},{24,28},{28,0},{1,5},{5... | collective-permute-start | bytes 1572872 | tf_op jit(solution)/shard_map/ppermute | solution.py:82
  171.0 9.5 %copy-start.9 = (bf16[64,4,2,512]{3,0,2,1:T(8,128)(2,1)}, bf16[64,4,2,512]{3,0,2,1:T(8,128)(2,1)S(1)}, u32[]{:S(2)}) copy-start(bf16[64,4,2,512]{3,0,2,1:T(8,128)(2,1)S(1)} %collective-permute-done) | copy-start | bytes 1572868
  171.0 9.5 %collective-permute-start.1 = (bf16[64,4,2,512]{3,0,2,1:T(8,128)(2,1)S(1)}, bf16[64,4,2,512]{3,0,2,1:T(8,128)(2,1)S(1)}, u32[]{:S(2)}, u32[]{:S(2)}) collective-permute-start(bf16[64,4,2,512]{3,0,2,1:T(8,128)(2,1)S(1)} %collective-permute-done), channel_id=1, source_target_pairs={{0,4},{4,8},{8,12},{12,16},{16,20},{20,24},{24,28},{28,0},{1,5},{5... | collective-permute-start | bytes 1572872 | tf_op jit(solution)/shard_map/ppermute | solution.py:82
  180.5 0.8 copy-start.11
  180.5 9.5 %collective-permute-start.2 = (bf16[64,4,2,512]{3,0,2,1:T(8,128)(2,1)S(1)}, bf16[64,4,2,512]{3,0,2,1:T(8,128)(2,1)S(1)}, u32[]{:S(2)}, u32[]{:S(2)}) collective-permute-start(bf16[64,4,2,512]{3,0,2,1:T(8,128)(2,1)S(1)} %collective-permute-done.1), channel_id=1, source_target_pairs={{0,4},{4,8},{8,12},{12,16},{16,20},{20,24},{24,28},{28,0},{1,5},{5... | collective-permute-start | bytes 1572872 | tf_op jit(solution)/shard_map/ppermute | solution.py:82
  190.0 0.8 copy-start.13
  190.8 9.6 %collective-permute-start.3 = (bf16[64,4,2,512]{3,0,2,1:T(8,128)(2,1)S(1)}, bf16[64,4,2,512]{3,0,2,1:T(8,128)(2,1)}, u32[]{:S(2)}, u32[]{:S(2)}) collective-permute-start(bf16[64,4,2,512]{3,0,2,1:T(8,128)(2,1)S(1)} %collective-permute-done.2), channel_id=1, source_target_pairs={{0,4},{4,8},{8,12},{12,16},{16,20},{20,24},{24,28},{28,0},{1,5},{5... | collective-permute-start | bytes 1572872 | tf_op jit(solution)/shard_map/ppermute | solution.py:82
  200.4 9.8 %collective-permute-start.4 = (bf16[64,4,2,512]{3,0,2,1:T(8,128)(2,1)}, bf16[64,4,2,512]{3,0,2,1:T(8,128)(2,1)}, u32[]{:S(2)}, u32[]{:S(2)}) collective-permute-start(bf16[64,4,2,512]{3,0,2,1:T(8,128)(2,1)} %collective-permute-done.3), channel_id=1, source_target_pairs={{0,4},{4,8},{8,12},{12,16},{16,20},{20,24},{24,28},{28,0},{1,5},{5... | collective-permute-start | bytes 1572872 | tf_op jit(solution)/shard_map/ppermute | solution.py:82
  200.4 12.3 %copy-start.2 = (bf16[512,4,384]{0,2,1:T(8,128)(2,1)S(1)}, bf16[512,4,384]{0,2,1:T(8,128)(2,1)}, u32[]{:S(2)}) copy-start(bf16[512,4,384]{0,2,1:T(8,128)(2,1)} %copy-done.1) | copy-start | bytes 4718596
  200.4 12.4 %copy-start.3 = (bf16[512,4,384]{0,2,1:T(8,128)(2,1)S(1)}, bf16[512,4,384]{0,2,1:T(8,128)(2,1)}, u32[]{:S(2)}) copy-start(bf16[512,4,384]{0,2,1:T(8,128)(2,1)} %get-tuple-element.4) | copy-start | bytes 4718596
  210.2 9.7 %collective-permute-start.5 = (bf16[64,4,2,512]{3,0,2,1:T(8,128)(2,1)}, bf16[64,4,2,512]{3,0,2,1:T(8,128)(2,1)S(1)}, u32[]{:S(2)}, u32[]{:S(2)}) collective-permute-start(bf16[64,4,2,512]{3,0,2,1:T(8,128)(2,1)} %collective-permute-done.4), channel_id=1, source_target_pairs={{0,4},{4,8},{8,12},{12,16},{16,20},{20,24},{24,28},{28,0},{1,5},{5... | collective-permute-start | bytes 1572872 | tf_op jit(solution)/shard_map/ppermute | solution.py:82
  212.8 7.4 %copy-start.7 = (f32[64,4,512]{2,0,1:T(8,128)S(1)}, f32[64,4,512]{2,0,1:T(8,128)}, u32[]{:S(2)}) copy-start(f32[64,4,512]{2,0,1:T(8,128)} %copy-done.6) | copy-start | bytes 1572868
  212.8 7.9 %copy-start.5 = (f32[64,4,512]{2,0,1:T(8,128)S(1)}, f32[64,4,512]{2,0,1:T(8,128)}, u32[]{:S(2)}) copy-start(f32[64,4,512]{2,0,1:T(8,128)} %copy-done.4) | copy-start | bytes 1572868
  212.8 8.5 %copy-start.8 = (f32[64,2,2,2,512]{4,3,2,1,0:T(2,128)S(1)}, f32[64,2,2,2,512]{4,3,2,1,0:T(2,128)}, u32[]{:S(2)}) copy-start(f32[64,2,2,2,512]{4,3,2,1,0:T(2,128)} %param.10) | copy-start | bytes 3145732
  219.9 9.5 %collective-permute-start.6 = (bf16[64,4,2,512]{3,0,2,1:T(8,128)(2,1)S(1)}, bf16[64,4,2,512]{3,0,2,1:T(8,128)(2,1)S(1)}, u32[]{:S(2)}, u32[]{:S(2)}) collective-permute-start(bf16[64,4,2,512]{3,0,2,1:T(8,128)(2,1)S(1)} %collective-permute-done.5), channel_id=1, source_target_pairs={{0,4},{4,8},{8,12},{12,16},{16,20},{20,24},{24,28},{28,0},{1,5},{5... | collective-permute-start | bytes 1572872 | tf_op jit(solution)/shard_map/ppermute | solution.py:82
  221.3 10.5 %copy-start.14 = (bf16[64,4,2,512]{3,0,2,1:T(8,128)(2,1)S(1)}, bf16[64,4,2,512]{3,0,2,1:T(8,128)(2,1)}, u32[]{:S(2)}) copy-start(bf16[64,4,2,512]{3,0,2,1:T(8,128)(2,1)} %copy-done.13) | copy-start | bytes 1572868
  221.3 10.5 %copy-start.12 = (bf16[64,4,2,512]{3,0,2,1:T(8,128)(2,1)S(1)}, bf16[64,4,2,512]{3,0,2,1:T(8,128)(2,1)}, u32[]{:S(2)}) copy-start(bf16[64,4,2,512]{3,0,2,1:T(8,128)(2,1)} %copy-done.11) | copy-start | bytes 1572868
  221.3 10.6 %copy-start.10 = (bf16[64,4,2,512]{3,0,2,1:T(8,128)(2,1)S(1)}, bf16[64,4,2,512]{3,0,2,1:T(8,128)(2,1)}, u32[]{:S(2)}) copy-start(bf16[64,4,2,512]{3,0,2,1:T(8,128)(2,1)} %copy-done.9) | copy-start | bytes 1572868
  234.4 3.3 %copy-start.15 = (bf16[1024,4,2,512]{3,0,2,1:T(8,128)(2,1)}, bf16[1024,4,2,512]{3,0,2,1:T(8,128)(2,1)S(1)}, u32[]{:S(2)}) copy-start(bf16[1024,4,2,512]{3,0,2,1:T(8,128)(2,1)S(1)} %constant_dynamic-update-slice_fusion) | copy-start | bytes 25165828
Sparse Core Ops, SparseCore 0:
  43.2 83.5 all-reduce.2
